TPU v7x, 32 devices: a whole 2x2x4 slice. The times are simulated.
32 devices in a mesh: dp: 8 (over z, core), tensor: 4 (over y, x).
Axes of the slice: x: 2, y: 2, z: 4, core: 2. Of those that a mesh axis runs over, the one named last changes fastest.
Arguments:
- token_ids: int32 [4096], P('dp'), may hold values from 0 to 511
- seq_lengths: int32 [16], P('dp'), may hold values from 32 to 256
- embed_table: bfloat16 [512, 8192], P('dp', 'tensor'), may hold values from -420 to 420
- norm_gain: float32 [8192], replicated, may hold values from 0.1 to 1.9
- query_weight: bfloat16 [8192, 8192], P('tensor', 'dp'), may hold values from -1.3479223 to 1.3479223
- kv_weight: bfloat16 [2048, 8192], P('tensor', 'dp'), may hold values from -0.044194174 to 0.044194174
Outputs:
- attention_out: bfloat16 [4096, 8192], P('dp', 'tensor')
All inputs are finite; a program needn't handle non-finite values.
Results may differ from a plain program's by a relative error of at most 0.0091.
Values may be sent and summed in bfloat16 or wider, within the bound.
A program may use at most 128 MiB of HBM per device.

v0:
```python
import math

import jax
import jax.numpy as jnp
from jax import lax
from jax.sharding import PartitionSpec as P

HD = 128
HEADS = 64
KV_HEADS = 8
SEQ = 256


epsilon = 1e-05
rope_base = 500000.0


def rope_tables(positions, head_size):
    halfway = head_size // 2
    frequencies = rope_base ** (-(jnp.arange(halfway, dtype=jnp.float32) * 2.0 / head_size))
    angles = positions.astype(jnp.float32)[:, None] * frequencies[None, :]
    return (jnp.cos(angles), jnp.sin(angles))


def rotate_last(values, cosine, sine_vals):
    halfway = values.shape[-1] // 2
    lower = values[..., :halfway]
    upper = values[..., halfway:]
    return jnp.concatenate(
        [lower * cosine - upper * sine_vals, upper * cosine + lower * sine_vals], axis=-1
    )


def rotate_middle(values, cosine_t, sine_t):
    halfway = values.shape[1] // 2
    lower = values[:, :halfway, :]
    upper = values[:, halfway:, :]
    return jnp.concatenate(
        [lower * cosine_t - upper * sine_t, upper * cosine_t + lower * sine_t], axis=1
    )


def on_device(token_ids, seq_lengths, embed_table, norm_gain, query_weight, kv_weight):
    tok_rows = token_ids.shape[0]
    tensor_index = lax.axis_index("tensor")
    tensor_count = lax.axis_size("tensor")
    table_part = lax.all_gather(embed_table, "dp", axis=0, tiled=True)
    vocab_size = table_part.shape[0]
    one_hot = (token_ids[:, None] == jnp.arange(vocab_size, dtype=jnp.int32)[None, :]).astype(
        jnp.bfloat16
    )
    embedded = jnp.dot(one_hot, table_part, preferred_element_type=jnp.float32)
    feature_width = embedded.shape[1]
    square_sum = lax.psum(jnp.sum(embedded * embedded, axis=1), "tensor")
    mean_square = square_sum / (feature_width * tensor_count)
    gain_part = lax.dynamic_slice_in_dim(norm_gain, tensor_index * feature_width, feature_width, 0)
    normed_part = (
        embedded * lax.rsqrt(mean_square[:, None] + epsilon) * gain_part[None, :]
    ).astype(jnp.bfloat16)
    normed = lax.all_gather(normed_part, "tensor", axis=1, tiled=True)
    columns = normed
    queries = lax.dot_general(
        columns,
        lax.all_gather(query_weight, "dp", axis=1, tiled=True),
        (((1,), (1,)), ((), ())),
        preferred_element_type=jnp.float32,
    )
    columns = normed
    keyvals_t = lax.dot_general(
        lax.all_gather(kv_weight, "dp", axis=1, tiled=True),
        columns,
        (((1,), (1,)), ((), ())),
        preferred_element_type=jnp.float32,
    )
    keyvals_all = lax.all_gather(keyvals_t.astype(jnp.bfloat16), "tensor", axis=0, tiled=True)
    heads_here = queries.shape[1] // HD
    group_size = HEADS // KV_HEADS
    kv_count = max(1, heads_here // group_size)
    per_group = heads_here // kv_count
    first_kv = tensor_index * heads_here // group_size
    seq_count = tok_rows // SEQ
    positions = jnp.arange(tok_rows, dtype=jnp.int32) % SEQ
    cosine, sine_vals = rope_tables(positions, HD)
    rot_queries = rotate_last(
        queries.reshape(tok_rows, heads_here, HD), cosine[:, None, :], sine_vals[:, None, :]
    ).astype(jnp.bfloat16)
    kv_grid = keyvals_all.reshape(2, KV_HEADS, HD, tok_rows)
    local_keys = lax.dynamic_slice_in_dim(kv_grid[0], first_kv, kv_count, 0)
    local_values = lax.dynamic_slice_in_dim(kv_grid[1], first_kv, kv_count, 0)
    rot_keys = rotate_middle(
        local_keys.astype(jnp.float32), cosine.T[None], sine_vals.T[None]
    ).astype(jnp.bfloat16)
    query_grid = rot_queries.reshape(seq_count, SEQ, kv_count, per_group, HD)
    key_grid = rot_keys.reshape(kv_count, HD, seq_count, SEQ)
    value_grid = local_values.reshape(kv_count, HD, seq_count, SEQ)
    scores = jnp.einsum(
        "sqghd,gdsk->sghqk", query_grid, key_grid, preferred_element_type=jnp.float32
    ) / math.sqrt(HD)
    slots = jnp.arange(SEQ, dtype=jnp.int32)
    causal = slots[None, :] <= slots[:, None]
    live = slots[None, :] < seq_lengths[:, None]
    allowed = causal[None, :, :] & live[:, None, :]
    scores = jnp.where(allowed[:, None, None, :, :], scores, -1e30)
    largest = jnp.max(scores, axis=-1, keepdims=True)
    exponent = jnp.exp(scores - largest)
    probs = (exponent / jnp.sum(exponent, axis=-1, keepdims=True)).astype(jnp.bfloat16)
    attended = jnp.einsum(
        "sghqk,gdsk->sqghd", probs, value_grid, preferred_element_type=jnp.float32
    )
    return attended.astype(jnp.bfloat16).reshape(tok_rows, heads_here * HD)


def solution(mesh):
    placed = (P("dp"), P("dp"), P("dp", "tensor"), P(), P("tensor", "dp"), P("tensor", "dp"))
    return jax.shard_map(
        on_device, mesh=mesh, in_specs=placed, out_specs=P("dp", "tensor"), check_vma=False
    )
```

profile of v0, /device:TPU:0, one launch (start us, length us, event | category | flops | bytes accessed | tf_op | source)
XLA Modules:
  0.0 602.2 jit_solution(15979382842780133080)
XLA Ops:
  8.1 32.8 %all-gather.6.cloned.1.call-done = bf16[512,2048]{1,0:T(8,128)(2,1)} async-done(((bf16[64,2048]{1,0:T(8,128)(2,1)}), bf16[512,2048]{1,0:T(8,128)(2,1)}) %all-gather.6.cloned.1.call-update) | async-done | bytes 2097168 | tf_op jit(solution)/shard_map/all_gather | solution.py:47
  40.8 4.9 multiply_reduce_fusion
  45.7 9.8 %psum.7 = f32[512]{0:T(512)S(1)} all-reduce(f32[512]{0:T(512)S(1)} %get-tuple-element.15), channel_id=1, replica_groups=mesh['dp'=8,'tensor'=4] {'tensor'}, use_global_device_ids=true, to_apply=%region_1.0 | all-reduce | flops 512 | bytes 4096 | tf_op jit(solution)/shard_map/psum | solution.py:54
  55.5 3.9 multiply_convert_fusion
  59.6 64.3 %all-gather.10.cloned.1.call-done = bf16[512,8192]{1,0:T(8,128)(2,1)} async-done(((bf16[512,1024]{1,0:T(8,128)(2,1)}), bf16[512,8192]{1,0:T(8,128)(2,1)}) %all-gather.10.cloned.1.call-update) | async-done | bytes 8388624 | tf_op jit(solution)/shard_map/all_gather | solution.py:70
  123.9 87.9 %all-gather.8.cloned.1.call-done = bf16[512,8192]{1,0:T(8,128)(2,1)} async-done(((bf16[512,2048]{1,0:T(8,128)(2,1)}), bf16[512,8192]{1,0:T(8,128)(2,1)}) %all-gather.8.cloned.1.call-update) | async-done | bytes 8388624 | tf_op jit(solution)/shard_map/all_gather | solution.py:60
  211.8 11.1 %fusion.10 = bf16[512,512]{0,1:T(8,128)(2,1)} fusion(bf16[512,8192]{1,0:T(8,128)(2,1)} %all-gather.8.cloned.1.call-done, bf16[512,8192]{1,0:T(8,128)(2,1)} %all-gather.10.cloned.1.call-done), kind=kOutput, calls=%fused_computation.19 | convolution fusion | flops 4295229440 | bytes 17301504 | tf_op jit(solution)/shard_map/dot_general | solution.py:69
  223.6 0.8 broadcast_and_fusion
  224.4 1.2 multiply_cosine_fusion
  226.2 31.9 %all-gather.12.cloned.1.call-done = bf16[2048,512]{0,1:T(8,128)(2,1)} async-done(((bf16[512,512]{0,1:T(8,128)(2,1)}), bf16[2048,512]{0,1:T(8,128)(2,1)}) %all-gather.12.cloned.1.call-update) | async-done | bytes 2097168 | tf_op jit(solution)/shard_map/all_gather | solution.py:75
  258.1 1.7 slice_bitcast_fusion
  260.8 0.9 copy.10
  263.0 285.2 %all-gather.14.cloned.1.call-done = bf16[2048,8192]{1,0:T(8,128)(2,1)} async-done(((bf16[2048,1024]{1,0:T(8,128)(2,1)}), bf16[2048,8192]{1,0:T(8,128)(2,1)}) %all-gather.14.cloned.1.call-update) | async-done | bytes 33554448 | tf_op jit(solution)/shard_map/all_gather | solution.py:64
  548.1 23.9 %fusion.24 = f32[512,2048]{0,1:T(8,128)S(1)} fusion(bf16[512,8192]{1,0:T(8,128)(2,1)} %all-gather.8.cloned.1.call-done, bf16[2048,8192]{1,0:T(8,128)(2,1)} %all-gather.14.cloned.1.call-done), kind=kOutput, calls=%fused_computation.51 | convolution fusion | flops 17179869184 | bytes 46137344 | tf_op jit(solution)/shard_map/reshape | solution.py:85
  572.0 0.8 subtract_convert_fusion
  572.8 1.1 concatenate.22
  573.9 2.8 copy.15
  576.8 1.1 concatenate.21
  577.9 4.0 copy.14
  581.8 3.3 fusion.6
  585.1 2.5 fusion.23
  587.6 2.3 convert_bitcast_fusion
  589.9 3.4 copy.18
  593.4 2.3 reshape.179
  (35 shorter events, 5.1 us)
Async XLA Ops:
  6.5 34.3 %all-gather.6.cloned.1.call-start = ((), (), s32[]{:S(2)}) async-start(), calls=%async_computation | async-start | bytes 2359296 | tf_op jit(solution)/shard_map/all_gather | solution.py:47
  7.3 116.6 %all-gather.10.cloned.1.call-start = ((), (), s32[]{:S(2)}) async-start(), calls=%async_computation.2 | async-start | bytes 9437184 | tf_op jit(solution)/shard_map/all_gather | solution.py:70
  8.0 203.7 %all-gather.8.cloned.1.call-start = ((), (), s32[]{:S(2)}) async-start(), calls=%async_computation.1 | async-start | bytes 10485760 | tf_op jit(solution)/shard_map/all_gather | solution.py:60
  8.1 47.5 %dynamic-slice-start = ((f32[8192]{0:T(1024)}, s32[]{:T(128)}), f32[2048]{0:T(1024)S(1)}, s32[]{:S(2)}) async-start(f32[8192]{0:T(1024)} %param.9, s32[]{:T(128)} %select_n.40), calls=%async_computation.5 | async-start | bytes 16896 | tf_op jit(solution)/shard_map/dynamic_slice | solution.py:56
  59.5 198.5 %all-gather.12.cloned.1.call-start = ((), (), s32[]{:S(2)}) async-start(), calls=%async_computation.3 | async-start | bytes 2621440 | tf_op jit(solution)/shard_map/all_gather | solution.py:75
  222.8 0.7 copy-start.3
  222.9 325.3 %all-gather.14.cloned.1.call-start = ((), (), s32[]{:S(2)}) async-start(), calls=%async_computation.4 | async-start | bytes 37748736 | tf_op jit(solution)/shard_map/all_gather | solution.py:64
  263.0 309.1 %copy-start = (f32[512,64]{0,1:T(8,128)S(1)}, f32[512,64]{0,1:T(8,128)}, u32[]{:S(2)}) copy-start(f32[512,64]{0,1:T(8,128)} %get-tuple-element.14) | copy-start | bytes 393220
  581.8 3.3 copy-start.2
  585.1 2.5 copy-start.1
Sparse Core Ops, SparseCore 0:
  8.9 31.8 all-gather.5
  42.4 81.4 all-gather.9
  125.8 85.9 all-gather.7
  223.0 35.0 all-gather.11
  259.5 288.5 all-gather.13
where the time goes:
time: 603 us; the launch traced here: 602 us
  waiting for transfers between devices  504 us (84%)
  matrix products  45.4 us (8%)
  local copies, waits for them, and re-layouts  19.5 us (3%)
  between operations  13.3 us (2%)
  other arithmetic  10 us (2%)
  blocking collectives  9.81 us (2%)
    all_gather x1, waiting for transfers between devices, on_device(): lax.all_gather(query_weight, 'dp', axis=1, tiled=True)  285 us
    all_gather x1, waiting for transfers between devices, on_device(): normed = lax.all_gather(normed_part, 'tensor', axis=1, tiled=True)  87.9 us
    all_gather x1, waiting for transfers between devices, on_device(): lax.all_gather(kv_weight, 'dp', axis=1, tiled=True)  64.3 us
    all_gather x1, waiting for transfers between devices, on_device(): table_part = lax.all_gather(embed_table, 'dp', axis=0, tiled=True)  32.8 us
    all_gather x1, waiting for transfers between devices, on_device(): lax.all_gather(keyvals_t.astype(jnp.bfloat16), 'tensor', axis=0, tiled=True)  31.9 us
    reshape x1, matrix products, on_device(): queries.reshape(tok_rows, heads_here, HD)  23.9 us
  transfers between devices with their start and end apart: 5, of which 5 were waited for; matrix products, arithmetic and copies ran while one was open for 3% of the time, Pallas kernels for 0%

commit v1 on v0

v1 whole, which is shorter than its diff:
```python
import math

import jax
import jax.numpy as jnp
from jax import lax
from jax.sharding import PartitionSpec as P

HD = 128
HEADS = 64
KV_HEADS = 8
SEQ = 256


epsilon = 1e-05
rope_base = 500000.0


def rope_tables(positions, head_size):
    halfway = head_size // 2
    frequencies = rope_base ** (-(jnp.arange(halfway, dtype=jnp.float32) * 2.0 / head_size))
    angles = positions.astype(jnp.float32)[:, None] * frequencies[None, :]
    return (jnp.cos(angles), jnp.sin(angles))


def rotate_last(values, cosine, sine_vals):
    halfway = values.shape[-1] // 2
    lower = values[..., :halfway]
    upper = values[..., halfway:]
    return jnp.concatenate(
        [lower * cosine - upper * sine_vals, upper * cosine + lower * sine_vals], axis=-1
    )


def on_device(token_ids, seq_lengths, embed_table, norm_gain, query_weight, kv_weight):
    tok_rows = token_ids.shape[0]
    tensor_index = lax.axis_index("tensor")
    tensor_count = lax.axis_size("tensor")
    heads_here = query_weight.shape[0] // HD
    group_size = HEADS // KV_HEADS
    kv_count = max(1, heads_here // group_size)
    per_group = heads_here // kv_count
    first_kv = tensor_index * heads_here // group_size
    rows = lax.all_gather(embed_table, "tensor", axis=1, tiled=True).astype(jnp.float32)
    mean_square = jnp.mean(rows * rows, axis=1, keepdims=True)
    normed_rows = (rows * lax.rsqrt(mean_square + epsilon) * norm_gain[None, :]).astype(jnp.bfloat16)
    normed = lax.all_to_all(normed_rows, "dp", split_axis=1, concat_axis=0, tiled=True)
    vocab_size = normed.shape[0]
    kv_grid = lax.all_gather(kv_weight, "tensor", axis=0, tiled=True).reshape(2, KV_HEADS, HD, -1)
    kv_rows = lax.dynamic_slice_in_dim(kv_grid, first_kv, kv_count, 1).reshape(2 * kv_count * HD, -1)
    weights = jnp.concatenate([query_weight, kv_rows], axis=0)
    partial = lax.dot_general(
        normed, weights, (((1,), (1,)), ((), ())), preferred_element_type=jnp.float32
    )
    summed = lax.psum_scatter(partial, "dp", scatter_dimension=0, tiled=True)
    table = lax.all_gather(summed.astype(jnp.bfloat16), "dp", axis=0, tiled=True)
    one_hot = (token_ids[:, None] == jnp.arange(vocab_size, dtype=jnp.int32)[None, :]).astype(
        jnp.bfloat16
    )
    picked = jnp.dot(one_hot, table, preferred_element_type=jnp.float32)
    q_width = heads_here * HD
    queries = picked[:, :q_width]
    seq_count = tok_rows // SEQ
    positions = jnp.arange(tok_rows, dtype=jnp.int32) % SEQ
    cosine, sine_vals = rope_tables(positions, HD)
    rot_queries = rotate_last(
        queries.reshape(tok_rows, heads_here, HD), cosine[:, None, :], sine_vals[:, None, :]
    ).astype(jnp.bfloat16)
    local = picked[:, q_width:].reshape(tok_rows, 2, kv_count, HD)
    rot_keys = rotate_last(
        local[:, 0], cosine[:, None, :], sine_vals[:, None, :]
    ).astype(jnp.bfloat16)
    query_grid = rot_queries.reshape(seq_count, SEQ, kv_count, per_group, HD)
    key_grid = rot_keys.reshape(seq_count, SEQ, kv_count, HD)
    value_grid = local[:, 1].astype(jnp.bfloat16).reshape(seq_count, SEQ, kv_count, HD)
    scores = jnp.einsum(
        "sqghd,skgd->sghqk", query_grid, key_grid, preferred_element_type=jnp.float32
    ) / math.sqrt(HD)
    slots = jnp.arange(SEQ, dtype=jnp.int32)
    causal = slots[None, :] <= slots[:, None]
    live = slots[None, :] < seq_lengths[:, None]
    allowed = causal[None, :, :] & live[:, None, :]
    scores = jnp.where(allowed[:, None, None, :, :], scores, -1e30)
    largest = jnp.max(scores, axis=-1, keepdims=True)
    exponent = jnp.exp(scores - largest)
    probs = (exponent / jnp.sum(exponent, axis=-1, keepdims=True)).astype(jnp.bfloat16)
    attended = jnp.einsum(
        "sghqk,skgd->sqghd", probs, value_grid, preferred_element_type=jnp.float32
    )
    return attended.astype(jnp.bfloat16).reshape(tok_rows, heads_here * HD)


def solution(mesh):
    placed = (P("dp"), P("dp"), P("dp", "tensor"), P(), P("tensor", "dp"), P("tensor", "dp"))
    return jax.shard_map(
        on_device, mesh=mesh, in_specs=placed, out_specs=P("dp", "tensor"), check_vma=False
    )
```

time: 603 us -> 244 us (0.40)
  waiting for transfers between devices: 504 us -> 169 us
  matrix products: 45.4 us -> 16.2 us
  blocking collectives: 9.81 us -> 0 us
  local copies, waits for them, and re-layouts: 19.5 us -> 28.8 us
    all_gather x5 -> x3, waiting for transfers between devices: 502 us -> 108 us  [the longest x1 45.6 us: on_device(): lax.all_gather(kv_weight, 'tensor', axis=0, tiled=True)]
    reduce_scatter x0 -> x1, waiting for transfers between devices: none -> 59.7 us  [on_device(): summed = lax.psum_scatter(partial, 'dp', scatter_dimension=0, tiled=True)]
    reshape x1 -> x0, matrix products: 23.9 us -> none  [on_device(): queries.reshape(tok_rows, heads_here, HD)]
    psum x1 -> x0, blocking collectives: 9.81 us -> none  [on_device(): square_sum = lax.psum(jnp.sum(embedded * embedded, axis=1), 'tensor')]
    reshape x0 -> x2, local copies, waits for them, and re-layouts: none -> 6.05 us  [the longest x1 5.38 us: on_device(): queries.reshape(tok_rows, heads_here, HD)]
  transfers between devices with their start and end apart: 5 -> 5, of which waited for: 5 -> 4; matrix products, arithmetic and copies ran while one was open for 3% -> 3% of each run, Pallas kernels for 0% -> 0%
where the time goes in v1:
time: 244 us; the launch traced here: 243 us
  waiting for transfers between devices  169 us (69%)
  local copies, waits for them, and re-layouts  28.8 us (12%)
  matrix products  16.2 us (7%)
  between operations  13.3 us (5%)
  other arithmetic  11.3 us (5%)
  starting transfers between devices  4.9 us (2%)
    reduce_scatter x1, waiting for transfers between devices, on_device(): summed = lax.psum_scatter(partial, 'dp', scatter_dimension=0, tiled=True)  59.7 us
    all_gather x1, waiting for transfers between devices, on_device(): lax.all_gather(kv_weight, 'tensor', axis=0, tiled=True)  45.6 us
    all_gather x1, waiting for transfers between devices, on_device(): lax.all_gather(summed.astype(jnp.bfloat16), 'dp', axis=0, tiled=True)  31.5 us
    all_gather x1, waiting for transfers between devices, on_device(): lax.all_gather(embed_table, 'tensor', axis=1, tiled=True)  30.4 us
    concatenate x8, local copies, waits for them, and re-layouts, rotate_last(): jnp.concatenate([lower * cosine - upper * sine_vals, upper * cosine + low...  10.1 us
    dot_general x1, matrix products, on_device(): lax.dot_general(normed, weights, (((1,), (1,)), ((), ())), preferred_elem...  7.4 us
    reshape x1, local copies, waits for them, and re-layouts, on_device(): queries.reshape(tok_rows, heads_here, HD)  5.38 us
  transfers between devices with their start and end apart: 5, of which 4 were waited for; matrix products, arithmetic and copies ran while one was open for 3% of the time, Pallas kernels for 0%

profile of v1, /device:TPU:0, one launch (start us, length us, event | category | flops | bytes accessed | tf_op | source)
XLA Modules:
  0.0 243.2 jit_solution(12173982191233598166)
XLA Ops:
  8.0 30.4 %all-gather.4.cloned.1.call-done = bf16[64,8192]{1,0:T(8,128)(2,1)} async-done(((bf16[64,2048]{1,0:T(8,128)(2,1)}), bf16[64,8192]{1,0:T(8,128)(2,1)}) %all-gather.4.cloned.1.call-update) | async-done | bytes 1048592 | tf_op jit(solution)/shard_map/all_gather | solution.py:43
  38.4 1.5 fusion.10
  40.0 1.5 fusion.12
  42.6 4.6 %all-to-all-start = ((bf16[64,8,1024]{2,0,1:T(8,128)(2,1)}), bf16[64,8,1024]{2,0,1:T(8,128)(2,1)S(1)}, u32[]{:S(2)}, u32[]{:S(2)}) async-start(bf16[64,8,1024]{2,0,1:T(8,128)(2,1)} %bitcast.43), calls=%async_computation | async-start | bytes 2097152 | tf_op jit(solution)/shard_map/all_to_all | solution.py:46
  47.3 45.6 %all-gather.6.cloned.1.call-done = bf16[2048,1024]{1,0:T(8,128)(2,1)} async-done(((bf16[512,1024]{1,0:T(8,128)(2,1)}), bf16[2048,1024]{1,0:T(8,128)(2,1)}) %all-gather.6.cloned.1.call-update) | async-done | bytes 4194320 | tf_op jit(solution)/shard_map/all_gather | solution.py:48
  92.9 1.3 constant_dynamic-slice_fusion
  94.2 7.4 %fusion.2 = f32[512,2560]{1,0:T(8,128)} fusion(bf16[512,1024]{1,0:T(8,128)(2,1)S(1)} %bitcast.48, bf16[512,1024]{1,0:T(8,128)(2,1)S(1)} %bitcast.47, bf16[2048,1024]{1,0:T(8,128)(2,1)} %param.10), kind=kOutput, calls=%fused_computation.5 | convolution fusion | flops 2694840320 | bytes 11534336 | tf_op jit(solution)/shard_map/dot_general | solution.py:51
  101.8 59.7 %reduce-scatter.2.cloned.1.call-done = f32[64,2560]{1,0:T(8,128)} async-done(((f32[512,2560]{1,0:T(8,128)}), f32[64,2560]{1,0:T(8,128)}) %reduce-scatter.2.cloned.1.call-update) | async-done | bytes 655376 | tf_op jit(solution)/shard_map/reduce_scatter | solution.py:54
  161.6 1.8 convert_element_type.51
  164.3 31.5 %all-gather.8.cloned.1.call-done = bf16[512,2560]{1,0:T(8,128)(2,1)} async-done(((bf16[64,2560]{1,0:T(8,128)(2,1)}), bf16[512,2560]{1,0:T(8,128)(2,1)}) %all-gather.8.cloned.1.call-update) | async-done | bytes 2621456 | tf_op jit(solution)/shard_map/all_gather | solution.py:55
  195.8 3.3 %fusion.17 = f32[512,2560]{1,0:T(8,128)S(1)} fusion(bf16[512,2560]{1,0:T(8,128)(2,1)} %all-gather.8.cloned.1.call-done, s32[512]{0:T(512)S(1)} %copy-done.3), kind=kOutput, calls=%fused_computation.27 | convolution fusion | flops 1342439424 | bytes 7866368 | tf_op jit(solution)/shard_map/dot_general | solution.py:59
  199.2 2.3 slice.38
  202.2 1.1 slice.34
  203.3 5.4 %copy.48 = f32[512,2048]{0,1:T(8,128)} copy(f32[512,2048]{1,0:T(8,128)} %slice.38) | data formatting | bytes 8388608 | tf_op jit(solution)/shard_map/reshape | solution.py:66
  208.7 3.0 %subtract_convert_fusion = (bf16[512,16,64]{0,2,1:T(8,128)(2,1)S(1)}, bf16[512,16,64]{0,2,1:T(8,128)(2,1)S(1)}) fusion(f32[512,16,128]{0,2,1:T(8,128)} %bitcast.44, f32[512,64]{0,1:T(8,128)S(1)} %get-tuple-element.10, f32[512,64]{0,1:T(8,128)S(1)} %get-tuple-element.9), kind=kLoop, calls=%fused_computation.24 | loop fusion | flops 4194304 | bytes 6553600 | tf_op jit(solution)/shard_map/convert.3
  211.7 1.1 concatenate.25
  215.0 2.8 %copy.38 = bf16[2,256,2,8,64]{4,1,3,2,0:T(8,128)(2,1)S(1)} copy(bf16[2,256,2,8,64]{1,0,4,3,2:T(2,128)(2,1)} %concatenate.25) | data formatting | bytes 2097152 | tf_op jit(solution)/shard_map/concatenate | solution.py:29
  217.9 1.1 concatenate.26
  219.0 4.0 %copy.39 = bf16[2,256,2,8,64]{4,1,3,2,0:T(8,128)(2,1)} copy(bf16[2,256,2,8,64]{1,0,4,3,2:T(2,128)(2,1)} %concatenate.26) | data formatting | bytes 2097152 | tf_op jit(solution)/shard_map/concatenate | solution.py:29
  222.9 3.2 %fusion.13 = f32[2,2,256,256,8]{3,2,4,1,0:T(8,128)S(1)} fusion(bf16[2,256,2,8,64]{4,1,3,2,0:T(8,128)(2,1)} %copy.39, bf16[2,256,2,8,64]{4,1,3,2,0:T(8,128)(2,1)S(1)} %copy.38, bf16[2,256,2,64]{3,1,2,0:T(8,128)(2,1)} %copy.35, bf16[2,256,2,64]{3,1,2,0:T(8,128)(2,1)S(1)} %copy.34), kind=kOutput, calls=%fused_computation.18 | convolution fusion | flops 541589504 | bytes 10747904 | tf_op jit(solution)/shard_map/sqghd,skgd->sghqk/dot_general | solution.py:75
  226.2 2.5 %fusion.30 = (f32[2,2,8,256]{3,2,1,0:T(8,128)S(1)}, f32[2,2,8,256,256]{3,4,2,1,0:T(8,128)S(1)}) fusion(f32[2,2,256,256,8]{3,2,4,1,0:T(8,128)S(1)} %fusion.13, pred[2,256,256]{1,2,0:T(8,128)(4,1)S(1)} %broadcast_and_fusion), kind=kOutput, calls=%fused_computation.54 | output fusion | flops 12583167 | bytes 16941056 | tf_op jit(solution)/shard_map/sub | solution.py:84
  228.7 2.3 convert_bitcast_fusion
  231.0 3.4 %copy.42 = bf16[2,256,2,8,128]{4,3,2,1,0:T(8,128)(2,1)S(1)} copy(bf16[2,256,2,8,128]{1,4,3,2,0:T(8,128)(2,1)} %convert_bitcast_fusion) | data formatting | bytes 4194304 | tf_op jit(solution)/shard_map/convert_element_type | solution.py:89
  234.4 2.3 reshape.140
  (38 shorter events, 6.5 us)
Async XLA Ops:
  6.5 31.9 %all-gather.4.cloned.1.call-start = ((), (), s32[]{:S(2)}) async-start(), calls=%async_computation.2 | async-start | bytes 1310720 | tf_op jit(solution)/shard_map/all_gather | solution.py:43
  7.3 85.6 %all-gather.6.cloned.1.call-start = ((), (), s32[]{:S(2)}) async-start(), calls=%async_computation.3 | async-start | bytes 5242880 | tf_op jit(solution)/shard_map/all_gather | solution.py:48
  42.6 51.6 %all-to-all-start = ((bf16[64,8,1024]{2,0,1:T(8,128)(2,1)}), bf16[64,8,1024]{2,0,1:T(8,128)(2,1)S(1)}, u32[]{:S(2)}, u32[]{:S(2)}) async-start(bf16[64,8,1024]{2,0,1:T(8,128)(2,1)} %bitcast.43), calls=%async_computation | async-start | bytes 2097152 | tf_op jit(solution)/shard_map/all_to_all | solution.py:46
  47.2 114.4 %reduce-scatter.2.cloned.1.call-start = ((), (), s32[]{:S(2)}) async-start(), calls=%async_computation.4 | async-start | bytes 5898240 | tf_op jit(solution)/shard_map/reduce_scatter | solution.py:54
  101.6 61.9 %copy-start.4 = (s32[2]{0:T(128)S(1)}, s32[2]{0:T(128)}, u32[]{:S(2)}) copy-start(s32[2]{0:T(128)} %param.7) | copy-start | bytes 28
  101.6 94.2 %copy-start.3 = (s32[512]{0:T(512)S(1)}, s32[512]{0:T(512)}, u32[]{:S(2)}) copy-start(s32[512]{0:T(512)} %param.6) | copy-start | bytes 6148
  101.6 94.2 %all-gather.8.cloned.1.call-start = ((), (), s32[]{:S(2)}) async-start(), calls=%async_computation.5 | async-start | bytes 2949120 | tf_op jit(solution)/shard_map/all_gather | solution.py:55
  202.2 6.5 %copy-start = (f32[512,2,2,128]{3,2,1,0:T(2,128)}, f32[512,2,2,128]{3,2,1,0:T(2,128)S(1)}, u32[]{:S(2)}) copy-start(f32[512,2,2,128]{3,2,1,0:T(2,128)S(1)} %reshape.138) | copy-start | bytes 3145732
  208.7 4.1 %slice-start = ((f32[512,2,2,128]{3,2,1,0:T(2,128)}), f32[512,1,2,128]{3,2,1,0:T(2,128)S(1)}, s32[]{:S(2)}) async-start(f32[512,2,2,128]{3,2,1,0:T(2,128)} %copy-done), calls=%async_computation.6 | async-start | bytes 1048576 | tf_op jit(solution)/shard_map/slice | solution.py:70
  208.7 4.5 %copy-start.1 = (bf16[512,1,2,128]{3,2,1,0:T(2,128)(2,1)S(1)}, bf16[512,1,2,128]{3,2,1,0:T(2,128)(2,1)}, u32[]{:S(2)}) copy-start(bf16[512,1,2,128]{3,2,1,0:T(2,128)(2,1)} %slice.34) | copy-start | bytes 786436
  226.2 2.5 %copy-start.2 = (bf16[512,1,2,128]{3,0,2,1:T(8,128)(2,1)S(1)}, bf16[512,1,2,128]{3,0,2,1:T(8,128)(2,1)}, u32[]{:S(2)}) copy-start(bf16[512,1,2,128]{3,0,2,1:T(8,128)(2,1)} %copy.56) | copy-start | bytes 786436
Sparse Core Ops, SparseCore 0:
  9.2 29.2 all-gather.3
  40.3 52.5 all-gather.5
  101.7 59.8 reduce-scatter.1
  163.6 32.1 all-gather.7

commit v2 on v1

v2 whole, which is shorter than its diff:
```python
import math

import functools

import jax
import jax.numpy as jnp
import numpy as np
from jax import lax
from jax.experimental import pallas as pl
from jax.experimental.pallas import tpu as pltpu
from jax.sharding import PartitionSpec as P

HD = 128
HEADS = 64
KV_HEADS = 8
SEQ = 256


epsilon = 1e-05
rope_base = 500000.0


MESH = pl.DeviceIdType.MESH
F32 = jnp.float32
BF16 = jnp.bfloat16
WIDE = 256


def rope_tables():
    halfway = HD // 2
    frequencies = np.float32(rope_base) ** (-(np.arange(halfway, dtype=np.float32) * np.float32(2.0) / np.float32(HD)))
    angles = np.arange(SEQ, dtype=np.float32)[:, None] * frequencies[None, :].astype(np.float32)
    cosine, sine = np.cos(angles), np.sin(angles)
    return (
        np.concatenate([cosine, cosine], axis=1).astype(np.float32),
        np.concatenate([-sine, sine], axis=1).astype(np.float32),
    )


def contract_last(left, right):
    return lax.dot_general(left, right, (((1,), (1,)), ((), ())), preferred_element_type=F32)


def attend_kernel(sub, tensor_count, per_dp, heads, len_ref, id_ref, cos_ref, sin_ref, q_ref, k_ref, v_ref, out_ref):
    length = len_ref[pl.program_id(0)]
    ids = id_ref[...]
    if sub:
        ids = ((ids % per_dp) // sub) * (q_ref.shape[1] // tensor_count) + (ids // per_dp) * sub + ids % sub
    vocab = q_ref.shape[1]
    one_hot = jnp.where(
        ids == lax.broadcasted_iota(jnp.int32, (SEQ, vocab), 1), 1.0, 0.0
    ).astype(BF16)
    cosine, sine = cos_ref[...], sin_ref[...]

    def rotate(x):
        return (x * cosine + pltpu.roll(x, HD // 2, 1) * sine).astype(BF16)

    keys = rotate(jnp.dot(one_hot, k_ref[0], preferred_element_type=F32))
    values = jnp.dot(one_hot, v_ref[0], preferred_element_type=F32).astype(BF16)
    row = lax.broadcasted_iota(jnp.int32, (SEQ, SEQ), 0)
    column = lax.broadcasted_iota(jnp.int32, (SEQ, SEQ), 1)
    allowed = (column <= row) & (column < length)
    for block in range(heads * HD // WIDE):
        picked = jnp.dot(one_hot, q_ref[block], preferred_element_type=F32)
        for inner in range(WIDE // HD):
            queries = rotate(picked[:, inner * HD : (inner + 1) * HD])
            scores = contract_last(queries, keys) * (1.0 / math.sqrt(HD))
            scores = jnp.where(allowed, scores, -1e30)
            exponent = jnp.exp(scores - jnp.max(scores, axis=1, keepdims=True))
            total = jnp.sum(exponent, axis=1, keepdims=True)
            probs = (exponent * (1.0 / total)).astype(BF16)
            start = block * WIDE + inner * HD
            out_ref[:, start : start + HD] = jnp.dot(
                probs, values, preferred_element_type=F32
            ).astype(BF16)


def table_kernel(
    T, DP, emb, gain, wq, kvw, out,
    rows_in, nrm, xt, wbuf, psend, pown, precv, zsend, zown, zrecv,
    w_sem, kv_send, kv_recv, e_send, e_recv, a_send, a_recv, x_send, x_recv,
    p_send, p_recv, z_send, z_recv, g_send, g_recv, f_send, f_recv,
):
    t = lax.axis_index("tensor")
    d = lax.axis_index("dp")
    Z = DP // 2
    z, core = d // 2, d % 2
    partner = d + 1 - 2 * core
    sub = nrm.shape[1]
    width = nrm.shape[2]
    per = rows_in.shape[2] // width
    nq = wq.shape[0]
    C = wbuf.shape[0]
    seg = zown.shape[1]

    def remote(src, dst, send, recv, **where):
        return pltpu.make_async_remote_copy(
            src_ref=src, dst_ref=dst, send_sem=send, recv_sem=recv, device_id=where, device_id_type=MESH
        )

    load_q = pltpu.make_async_copy(wq, wbuf.at[pl.ds(0, nq)], w_sem)
    load_q.start()

    barrier = pltpu.get_barrier_semaphore()
    for o in range(1, T):
        pl.semaphore_signal(barrier, inc=1, device_id={"tensor": (t + o) % T}, device_id_type=MESH)
    for o in range(1, DP):
        pl.semaphore_signal(barrier, inc=1, device_id={"dp": (d + o) % DP}, device_id_type=MESH)
    pl.semaphore_wait(barrier, T - 1 + DP - 1)

    def e_copy(o):
        p = (t + o) % T
        return remote(
            emb.at[pl.ds(pl.multiple_of(p * sub, sub), sub)], rows_in.at[t], e_send.at[o - 1], e_recv.at[o - 1], tensor=p
        )

    for o in range(1, T):
        e_copy(o).start()

    need = kvw.shape[0] * T // 2 // T
    half = T // 2
    spread = kvw.shape[0] // need
    slot = t // half

    def kv_part(p):
        return kvw.at[pl.ds(pl.multiple_of((p % spread) * need, need), need)]

    def kv_copy(p):
        return remote(kv_part(p), wbuf.at[nq + slot], kv_send.at[p % spread], kv_recv.at[slot], tensor=p)

    for o in range(1, T):
        p = (t + o) % T

        @pl.when(p // spread == t % half)
        def _():
            kv_copy(p).start()

    @pl.when(t // spread == t % half)
    def _():
        pltpu.make_async_copy(kv_part(t), wbuf.at[nq + slot], kv_recv.at[slot]).start()

    rows_in[t] = emb[pl.ds(pl.multiple_of(t * sub, sub), sub), :]
    for o in range(1, T):
        e_copy(o).wait_recv()
    total = jnp.zeros((sub, 1), F32)
    for k in range(T):
        x = rows_in[k].astype(F32)
        total = total + jnp.sum(x * x, axis=1, keepdims=True)
    scale = lax.rsqrt(total / (DP * width) + epsilon)
    for k in range(DP):
        x = rows_in[k // per, :, (k % per) * width : (k % per + 1) * width].astype(F32)
        nrm[k] = (x * scale * gain[:, k * width : (k + 1) * width]).astype(BF16)

    def a_copy(o):
        p = (d + o) % DP
        return remote(nrm.at[p], xt.at[t, d], a_send.at[o - 1], a_recv.at[o - 1], dp=p)

    for o in range(1, DP):
        a_copy(o).start()
    xt[t, d] = nrm[d]

    def x_copy(o, piece):
        source = (d + DP - piece) % DP
        return remote(
            nrm.at[d] if piece == 0 else xt.at[t, source], xt.at[t, source], x_send.at[o - 1, piece], x_recv.at[o - 1, piece],
            tensor=(t + o) % T,
        )

    for piece in range(DP):
        if piece:
            a_copy(piece).wait_recv()
        for o in range(1, T):
            x_copy(o, piece).start()

    load_q.wait()
    for k in range(2):
        pltpu.make_async_copy(wbuf.at[nq + k], wbuf.at[nq + k], kv_recv.at[k]).wait()
    for piece in range(DP):
        for o in range(1, T):
            x_copy(o, piece).wait_recv()

    def half_rows(which):
        return xt[pl.ds(which * half, half)].reshape(Z * seg, width)

    def p_copy(c):
        return remote(psend.at[c], precv.at[c], p_send.at[c], p_recv.at[c], dp=partner)

    def z_copy(o, c):
        there = (z + o) % Z
        return remote(
            zsend.at[c, there], zrecv.at[o - 1, c], z_send.at[o - 1, c], z_recv.at[o - 1, c], dp=there * 2 + core
        )

    def matmuls(c, _):
        psend[c] = contract_last(half_rows(1 - core), wbuf[c])
        p_copy(c).start()
        pown[c] = contract_last(half_rows(core), wbuf[c])
        return 0

    def pair_sums(c, _):
        p_copy(c).wait_recv()
        both = (pown[c] + precv[c]).reshape(Z, seg, WIDE)
        zsend[c] = both.astype(BF16)
        for o in range(1, Z):
            z_copy(o, c).start()
        pown[c] = both.reshape(Z * seg, WIDE)
        zown[c] = pown[c, pl.ds(pl.multiple_of(z * seg, seg), seg), :]
        return 0

    def matmul_then_pair(c, _):
        matmuls(c, 0)
        return pair_sums(c - 1, 0)

    matmuls(0, 0)
    lax.fori_loop(1, C, matmul_then_pair, 0)
    pair_sums(C - 1, 0)

    def chunk(c, which_core, which_z):
        return out.at[c, pl.ds(pl.multiple_of((which_core * Z + which_z) * seg, seg), seg)]

    def g_copy(o, c):
        mine = chunk(c, core, z)
        return remote(mine, mine, g_send.at[o - 1, c], g_recv.at[o - 1, c], dp=((z + o) % Z) * 2 + core)

    def f_copy(o, c):
        piece = chunk(c, core, (z + Z - o) % Z)
        return remote(piece, piece, f_send.at[o, c], f_recv.at[o, c], dp=partner)

    def finish(c, _):
        acc = zown[c]
        for o in range(1, Z):
            z_copy(o, c).wait_recv()
            acc = acc + zrecv[o - 1, c].astype(F32)
        out[c, pl.ds(pl.multiple_of((core * Z + z) * seg, seg), seg), :] = acc.astype(BF16)
        for o in range(1, Z):
            g_copy(o, c).start()
        f_copy(0, c).start()
        return 0

    lax.fori_loop(0, C, finish, 0)

    def forward(c, _):
        for o in range(1, Z):
            g_copy(o, c).wait_recv()
            f_copy(o, c).start()
        return 0

    lax.fori_loop(0, C, forward, 0)

    def drain(c, _):
        for o in range(Z):
            f_copy(o, c).wait()
        p_copy(c).wait_send()
        for o in range(1, Z):
            z_copy(o, c).wait_send()
            g_copy(o, c).wait_send()
        return 0

    lax.fori_loop(0, C, drain, 0)
    for o in range(1, T):
        e_copy(o).wait_send()
        p = (t + o) % T

        @pl.when(p // spread == t % half)
        def _():
            kv_copy(p).wait_send()

        for piece in range(DP):
            x_copy(o, piece).wait_send()
    for o in range(1, DP):
        a_copy(o).wait_send()


def table_by_kernel(embed_table, norm_gain, query_weight, kv_weight):
    T, DP = lax.axis_size("tensor"), lax.axis_size("dp")
    vocab = embed_table.shape[0] * DP
    width = query_weight.shape[1]
    sub = embed_table.shape[0] // T
    nq = query_weight.shape[0] // WIDE
    C = nq + 2
    Z = DP // 2
    seg = vocab // DP
    dma = pltpu.SemaphoreType.DMA
    return pl.pallas_call(
        functools.partial(table_kernel, T, DP),
        out_shape=jax.ShapeDtypeStruct((C, vocab, WIDE), BF16),
        in_specs=[
            pl.BlockSpec(memory_space=pltpu.VMEM),
            pl.BlockSpec(memory_space=pltpu.VMEM),
            pl.BlockSpec(memory_space=pl.ANY),
            pl.BlockSpec(memory_space=pl.ANY),
        ],
        out_specs=pl.BlockSpec(memory_space=pltpu.VMEM),
        scratch_shapes=[
            pltpu.VMEM((T, sub, embed_table.shape[1]), BF16),
            pltpu.VMEM((DP, sub, width), BF16),
            pltpu.VMEM((T, DP, sub, width), BF16),
            pltpu.VMEM((C, WIDE, width), BF16),
            pltpu.VMEM((C, Z * seg, WIDE), F32),
            pltpu.VMEM((C, Z * seg, WIDE), F32),
            pltpu.VMEM((C, Z * seg, WIDE), F32),
            pltpu.VMEM((C, Z, seg, WIDE), BF16),
            pltpu.VMEM((C, seg, WIDE), F32),
            pltpu.VMEM((Z - 1, C, seg, WIDE), BF16),
            dma(()), dma((2,)), dma((2,)),
            dma((T - 1,)), dma((T - 1,)), dma((DP - 1,)), dma((DP - 1,)),
            dma((T - 1, DP)), dma((T - 1, DP)),
            dma((C,)), dma((C,)), dma((Z - 1, C)), dma((Z - 1, C)),
            dma((Z - 1, C)), dma((Z - 1, C)), dma((Z, C)), dma((Z, C)),
        ],
        compiler_params=pltpu.CompilerParams(
            collective_id=0, has_side_effects=True, vmem_limit_bytes=48 * 1024 * 1024
        ),
        name="vocab_table",
    )(embed_table, norm_gain[None, :], query_weight.reshape(nq, WIDE, width), kv_weight)


def table_by_collectives(embed_table, norm_gain, query_weight, kv_weight, first_kv, kv_count):
    rows = lax.all_gather(embed_table, "tensor", axis=1, tiled=True).astype(F32)
    mean_square = jnp.mean(rows * rows, axis=1, keepdims=True)
    normed_rows = (rows * lax.rsqrt(mean_square + epsilon) * norm_gain[None, :]).astype(BF16)
    normed = lax.all_to_all(normed_rows, "dp", split_axis=1, concat_axis=0, tiled=True)
    kv_grid = lax.all_gather(kv_weight, "tensor", axis=0, tiled=True).reshape(2, KV_HEADS, HD, -1)
    kv_rows = lax.dynamic_slice_in_dim(kv_grid, first_kv, kv_count, 1).reshape(2, kv_count * HD, -1)
    kv_rows = jnp.pad(kv_rows, ((0, 0), (0, -kv_count * HD % WIDE), (0, 0))).reshape(-1, kv_rows.shape[2])
    weights = jnp.concatenate([query_weight, kv_rows], axis=0)
    summed = lax.psum_scatter(contract_last(normed, weights), "dp", scatter_dimension=0, tiled=True)
    table = lax.all_gather(summed.astype(BF16), "dp", axis=0, tiled=True)
    return table.reshape(table.shape[0], -1, WIDE).transpose(1, 0, 2)


def on_device(token_ids, seq_lengths, embed_table, norm_gain, query_weight, kv_weight):
    tok_rows = token_ids.shape[0]
    tensor_count, dp_count = lax.axis_size("tensor"), lax.axis_size("dp")
    heads_here = query_weight.shape[0] // HD
    group_size = HEADS // KV_HEADS
    kv_count = max(1, heads_here // group_size)
    per_dp = embed_table.shape[0]
    vocab = per_dp * dp_count
    sub = per_dp // tensor_count
    if sub % 16 == 0 and kv_count * HD == WIDE and tensor_count % 2 == 0 and dp_count % 2 == 0:
        table = table_by_kernel(embed_table, norm_gain, query_weight, kv_weight)
    else:
        sub = 0
        first_kv = lax.axis_index("tensor") * heads_here // group_size
        table = table_by_collectives(embed_table, norm_gain, query_weight, kv_weight, first_kv, kv_count)
    heads = min(4, heads_here)
    blocks = heads * HD // WIDE
    nq = heads_here * HD // WIDE
    nkv = kv_count * HD // WIDE if kv_count * HD >= WIDE else 1
    per_group = heads_here // kv_count
    lanes = WIDE // HD
    cosine, sine = rope_tables()
    whole = pl.BlockSpec((SEQ, HD), lambda s, j: (0, 0))

    def kv_spec(which):
        def index(s, j):
            group = j * heads // per_group
            return (nq + which * nkv + group // lanes, 0, group % lanes)

        return pl.BlockSpec((1, vocab, HD), index)

    return pl.pallas_call(
        functools.partial(attend_kernel, sub, tensor_count, per_dp, heads),
        grid=(tok_rows // SEQ, heads_here // heads),
        out_shape=jax.ShapeDtypeStruct((tok_rows, heads_here * HD), BF16),
        in_specs=[
            pl.BlockSpec(memory_space=pltpu.SMEM),
            pl.BlockSpec((SEQ, 1), lambda s, j: (s, 0)),
            whole,
            whole,
            pl.BlockSpec((blocks, vocab, WIDE), lambda s, j: (j, 0, 0)),
            kv_spec(0),
            kv_spec(1),
        ],
        out_specs=pl.BlockSpec((SEQ, heads * HD), lambda s, j: (s, j)),
        name="attend",
    )(seq_lengths, token_ids[:, None], cosine, sine, table, table, table)


def solution(mesh):
    placed = (P("dp"), P("dp"), P("dp", "tensor"), P(), P("tensor", "dp"), P("tensor", "dp"))
    return jax.shard_map(
        on_device, mesh=mesh, in_specs=placed, out_specs=P("dp", "tensor"), check_vma=False
    )
```

time: 244 us -> 119 us (0.49)
  waiting for transfers between devices: 169 us -> 0 us
  Pallas kernels: 0 us -> 113 us
  local copies, waits for them, and re-layouts: 28.8 us -> 5.96 us
  matrix products: 16.2 us -> 0 us
  between operations: 13.3 us -> 0.02 us
  other arithmetic: 11.3 us -> 0 us
  starting transfers between devices: 4.9 us -> 0 us
    pallas_call x0 -> x2, Pallas kernels: none -> 113 us  [the longest x1 96.3 us: table_by_kernel(): pl.pallas_call(functools.partial(table_kernel, T, DP), out_shape=jax.Shap...]
    all_gather x3 -> x0, waiting for transfers between devices: 108 us -> none  [the longest x1 45.6 us: on_device(): lax.all_gather(kv_weight, 'tensor', axis=0, tiled=True)]
    reduce_scatter x1 -> x0, waiting for transfers between devices: 59.7 us -> none  [on_device(): summed = lax.psum_scatter(partial, 'dp', scatter_dimension=0, tiled=True)]
    dot_general x4 -> x0, matrix products: 16.2 us -> none  [the longest x1 7.4 us: on_device(): lax.dot_general(normed, weights, (((1,), (1,)), ((), ())), preferred_elem...]
    concatenate x8 -> x0, local copies, waits for them, and re-layouts: 10.1 us -> none  [rotate_last(): jnp.concatenate([lower * cosine - upper * sine_vals, upper * cosine + low...]
    reshape x3 -> x0, local copies, waits for them, and re-layouts: 8.34 us -> none  [the longest x1 5.38 us: on_device(): queries.reshape(tok_rows, heads_here, HD)]
    all_to_all x1 -> x0, starting transfers between devices: 4.61 us -> none  [on_device(): lax.all_to_all(normed_rows, 'dp', split_axis=1, concat_axis=0, tiled=True)]
    slice x5 -> x0, local copies, waits for them, and re-layouts: 3.53 us -> none  [the longest x1 2.32 us: on_device(): queries = picked[:, :q_width]]
  transfers between devices with their start and end apart: 5 -> 0, of which waited for: 4 -> 0; matrix products, arithmetic and copies ran while one was open for 3% -> 0% of each run, Pallas kernels for 0% -> 0%
where the time goes in v2:
time: 119 us
  Pallas kernels  113 us (95%)
  local copies, waits for them, and re-layouts  5.96 us (5%)
    pallas_call x1, Pallas kernels, table_by_kernel(): pl.pallas_call(functools.partial(table_kernel, T, DP), out_shape=jax.Shap...  96.3 us
    pallas_call x1, Pallas kernels, on_device(): pl.pallas_call(functools.partial(attend_kernel, sub, tensor_count, per_dp...  16.9 us
    unnamed x8, local copies, waits for them, and re-layouts  4.43 us

profile of v2, /device:TPU:0, one launch (start us, length us, event | category | flops | bytes accessed | tf_op | source)
XLA Modules:
  0.0 119.2 jit_solution(15165264674066168515)
XLA Ops:
  0.0 1.5 %copy.9.id_ref = s32[512,1]{1,0:T(8,128)} copy(s32[512,1]{0,1:T(1,128)} %bitcast.5) | data formatting | bytes 4096 | tf_op jit(solution)/shard_map/broadcast_in_dim | solution.py:378
  1.5 0.0 copy-start.1
  1.5 1.2 %copy-done.1 = bf16[512,1024]{1,0:T(8,128)(2,1)S(1)} copy-done((bf16[512,1024]{1,0:T(8,128)(2,1)S(1)}, bf16[512,1024]{1,0:T(8,128)(2,1)}, u32[]{:S(2)}) %copy-start.1) | copy-done | bytes 1048600
  2.8 0.0 copy-start.2
  2.8 0.9 copy-done.2
  3.7 0.0 copy-start.3
  3.7 0.8 copy-done.3
  4.5 96.3 %vocab_table.1.q_ref.k_ref.v_ref = bf16[10,512,256]{2,1,0:T(8,128)(2,1)S(1)} custom-call(bf16[64,2048]{1,0:T(8,128)(2,1)S(1)} %copy-done.2, f32[1,8192]{1,0:T(1,128)S(1)} %bitcast.3, bf16[8,256,1024]{2,1,0:T(8,128)(2,1)} %bitcast.4, bf16[512,1024]{1,0:T(8,128)(2,1)S(1)} %copy-done.1), custom_call_target="tpu_custom_call" | custom-call | tf_op jit(solution)/shard_map/vocab_table/pallas_call | solution.py:284
  100.7 0.0 copy-start
  100.8 1.5 %copy-done = bf16[10,512,256]{2,1,0:T(8,128)(2,1)} copy-done((bf16[10,512,256]{2,1,0:T(8,128)(2,1)}, bf16[10,512,256]{2,1,0:T(8,128)(2,1)S(1)}, u32[]{:S(2)}) %copy-start) | copy-done | bytes 2621464
  102.2 16.9 %attend.1 = bf16[512,2048]{1,0:T(8,128)(2,1)} custom-call(s32[2]{0:T(128)} %len_ref.1, s32[512,1]{1,0:T(8,128)} %copy.9.id_ref, f32[256,128]{1,0:T(8,128)} %constant.4.clone.cos_ref, f32[256,128]{1,0:T(8,128)} %constant.5.clone.sin_ref, bf16[10,512,256]{2,1,0:T(8,128)(2,1)} %copy-done, bf16[10,512,256]{2,1,0:T(8,128)(2,1)} %copy-done, ...), custom_call_target="tpu_custom_call" | custom-call | tf_op jit(solution)/shard_map/attend/pallas_call | solution.py:363
Async XLA Ops:
  1.5 1.2 %copy-start.1 = (bf16[512,1024]{1,0:T(8,128)(2,1)S(1)}, bf16[512,1024]{1,0:T(8,128)(2,1)}, u32[]{:S(2)}) copy-start(bf16[512,1024]{1,0:T(8,128)(2,1)} %kvw.1) | copy-start | bytes 3145732
  2.8 0.9 copy-start.2
  3.7 0.8 copy-start.3
  100.7 1.5 %copy-start = (bf16[10,512,256]{2,1,0:T(8,128)(2,1)}, bf16[10,512,256]{2,1,0:T(8,128)(2,1)S(1)}, u32[]{:S(2)}) copy-start(bf16[10,512,256]{2,1,0:T(8,128)(2,1)S(1)} %vocab_table.1.q_ref.k_ref.v_ref) | copy-start | bytes 7864324

commit v3 on v2

v3 whole, which is shorter than its diff:
```python
import math

import functools

import jax
import jax.numpy as jnp
import numpy as np
from jax import lax
from jax.experimental import pallas as pl
from jax.experimental.pallas import tpu as pltpu
from jax.sharding import PartitionSpec as P

HD = 128
HEADS = 64
KV_HEADS = 8
SEQ = 256


epsilon = 1e-05
rope_base = 500000.0


MESH = pl.DeviceIdType.MESH
F32 = jnp.float32
BF16 = jnp.bfloat16
WIDE = 256


def rope_tables():
    halfway = HD // 2
    frequencies = np.float32(rope_base) ** (-(np.arange(halfway, dtype=np.float32) * np.float32(2.0) / np.float32(HD)))
    angles = np.arange(SEQ, dtype=np.float32)[:, None] * frequencies[None, :].astype(np.float32)
    cosine, sine = np.cos(angles), np.sin(angles)
    return (
        np.concatenate([cosine, cosine], axis=1).astype(np.float32),
        np.concatenate([-sine, sine], axis=1).astype(np.float32),
    )


def contract_last(left, right):
    return lax.dot_general(left, right, (((1,), (1,)), ((), ())), preferred_element_type=F32)


def attend_kernel(sub, tensor_count, per_dp, heads, nkv, len_ref, id_ref, cos_ref, sin_ref, table, out_ref, picker):
    length = len_ref[pl.program_id(0)]
    vocab = table.shape[1]

    @pl.when(pl.program_id(1) == 0)
    def _():
        ids = id_ref[0]
        if sub:
            ids = ((ids % per_dp) // sub) * (vocab // tensor_count) + (ids // per_dp) * sub + ids % sub
        hits = jnp.where(ids == lax.broadcasted_iota(jnp.int32, (vocab, SEQ), 0), 1.0, 0.0)
        picker[...] = hits.T.astype(BF16)

    one_hot = picker[...]
    group = pl.program_id(1)
    lane = pl.ds(pl.multiple_of(group % (WIDE // HD) * HD, HD), HD)
    part = group // (WIDE // HD)
    cosine, sine = cos_ref[...], sin_ref[...]

    def rotate(x):
        return (x * cosine + pltpu.roll(x, HD // 2, 1) * sine).astype(BF16)

    keys = rotate(jnp.dot(one_hot, table[part, :, lane], preferred_element_type=F32))
    values = jnp.dot(one_hot, table[nkv + part, :, lane], preferred_element_type=F32).astype(BF16)
    row = lax.broadcasted_iota(jnp.int32, (SEQ, SEQ), 0)
    column = lax.broadcasted_iota(jnp.int32, (SEQ, SEQ), 1)
    allowed = (column <= row) & (column < length)
    for block in range(heads * HD // WIDE):
        picked = jnp.dot(one_hot, table[2 * nkv + group * (heads * HD // WIDE) + block], preferred_element_type=F32)
        for inner in range(WIDE // HD):
            queries = rotate(picked[:, inner * HD : (inner + 1) * HD])
            scores = contract_last(queries, keys) * (1.0 / math.sqrt(HD))
            scores = jnp.where(allowed, scores, -1e30)
            exponent = jnp.exp(scores - jnp.max(scores, axis=1, keepdims=True))
            total = jnp.sum(exponent, axis=1, keepdims=True)
            probs = (exponent * (1.0 / total)).astype(BF16)
            start = block * WIDE + inner * HD
            out_ref[:, start : start + HD] = jnp.dot(
                probs, values, preferred_element_type=F32
            ).astype(BF16)


def table_kernel(
    T, DP, emb_in, gain_in, wq, kvw, out,
    emb, gain, rows_in, nrm, xt, wbuf, psend, pown, precv, zsend, right, left, kvout,
    w_sem, e_send, e_recv, a_send, a_recv, x_send, x_recv,
    p_send, p_recv, r_send, r_recv, l_send, l_recv, k_send, k_recv, g_send, g_recv, f_send, f_recv,
):
    t = lax.axis_index("tensor")
    d = lax.axis_index("dp")
    Z = DP // 2
    z, core = d // 2, d % 2
    partner = d + 1 - 2 * core
    sub = nrm.shape[1]
    width = nrm.shape[2]
    per = rows_in.shape[2] // width
    nq = wq.shape[0]
    nkv = kvw.shape[0]
    C = wbuf.shape[0]
    seg = kvout.shape[1]

    def remote(src, dst, send, recv, **where):
        return pltpu.make_async_remote_copy(
            src_ref=src, dst_ref=dst, send_sem=send, recv_sem=recv, device_id=where, device_id_type=MESH
        )

    loads = (
        pltpu.make_async_copy(emb_in, emb, w_sem.at[0]),
        pltpu.make_async_copy(gain_in, gain, w_sem.at[1]),
        pltpu.make_async_copy(kvw, wbuf.at[pl.ds(0, nkv)], w_sem.at[2]),
        pltpu.make_async_copy(wq, wbuf.at[pl.ds(nkv, nq)], w_sem.at[3]),
    )
    for load in loads:
        load.start()

    barrier = pltpu.get_barrier_semaphore()
    for o in range(1, T):
        pl.semaphore_signal(barrier, inc=1, device_id={"tensor": (t + o) % T}, device_id_type=MESH)
    for o in range(1, DP):
        pl.semaphore_signal(barrier, inc=1, device_id={"dp": (d + o) % DP}, device_id_type=MESH)
    loads[0].wait()
    loads[1].wait()
    pl.semaphore_wait(barrier, T - 1 + DP - 1)

    def e_copy(o):
        p = (t + o) % T
        return remote(
            emb.at[pl.ds(pl.multiple_of(p * sub, sub), sub)], rows_in.at[t], e_send.at[o - 1], e_recv.at[o - 1], tensor=p
        )

    for o in range(1, T):
        e_copy(o).start()
    rows_in[t] = emb[pl.ds(pl.multiple_of(t * sub, sub), sub), :]
    for o in range(1, T):
        e_copy(o).wait_recv()
    total = jnp.zeros((sub, 1), F32)
    for k in range(T):
        x = rows_in[k].astype(F32)
        total = total + jnp.sum(x * x, axis=1, keepdims=True)
    scale = lax.rsqrt(total / (DP * width) + epsilon)
    for k in range(DP):
        x = rows_in[k // per, :, (k % per) * width : (k % per + 1) * width].astype(F32)
        nrm[k] = (x * scale * gain[:, k * width : (k + 1) * width]).astype(BF16)

    def a_copy(o):
        p = (d + o) % DP
        return remote(nrm.at[p], xt.at[t, d], a_send.at[o - 1], a_recv.at[o - 1], dp=p)

    for o in range(1, DP):
        a_copy(o).start()
    xt[t, d] = nrm[d]

    def x_copy(o, piece):
        source = (d + DP - piece) % DP
        return remote(
            nrm.at[d] if piece == 0 else xt.at[t, source], xt.at[t, source], x_send.at[o - 1, piece], x_recv.at[o - 1, piece],
            tensor=(t + o) % T,
        )

    for piece in range(DP):
        if piece:
            a_copy(piece).wait_recv()
        for o in range(1, T):
            x_copy(o, piece).start()

    loads[2].wait()
    loads[3].wait()
    for piece in range(DP):
        for o in range(1, T):
            x_copy(o, piece).wait_recv()

    half = T // 2

    def half_rows(which):
        return xt[pl.ds(which * half, half)].reshape(Z * seg, width)

    def p_copy(c):
        return remote(psend.at[c], precv.at[c], p_send.at[c], p_recv.at[c], dp=partner)

    def r_copy(c, k):
        return remote(zsend.at[c, k], right.at[c, k], r_send.at[c, k], r_recv.at[c, k], dp=(z + 1) % Z * 2 + core)

    def l_copy(c, k):
        return remote(zsend.at[c, k], left.at[c, k], l_send.at[c, k], l_recv.at[c, k], dp=(z + Z - 1) % Z * 2 + core)

    def matmuls(c):
        psend[c] = contract_last(half_rows(1 - core), wbuf[c])
        p_copy(c).start()
        pown[c] = contract_last(half_rows(core), wbuf[c]).reshape(Z, seg, WIDE)

    def pair_sums(c):
        p_copy(c).wait_recv()
        pown[c] = pown[c] + precv[c].reshape(Z, seg, WIDE)

        @pl.when(z == 0)
        def _():
            for k in range(Z - 1, 0, -1):
                zsend[c, k] = pown[c, k].astype(BF16)
                r_copy(c, k).start()

        @pl.when(z == Z - 1)
        def _():
            for k in range(Z - 1):
                zsend[c, k] = pown[c, k].astype(BF16)
                l_copy(c, k).start()

    def relay(place):
        def run(c):
            @pl.when(z == place)
            def _():
                for k in range(Z - 1, place, -1):
                    r_copy(c, k).wait_recv()
                    zsend[c, k] = (pown[c, k] + right[c, k].astype(F32)).astype(BF16)
                    r_copy(c, k).start()

            @pl.when(z == Z - 1 - place)
            def _():
                for k in range(Z - 1 - place):
                    l_copy(c, k).wait_recv()
                    zsend[c, k] = (pown[c, k] + left[c, k].astype(F32)).astype(BF16)
                    l_copy(c, k).start()

        return run

    def chunk(c, which_core, which_z):
        return out.at[c, pl.ds(pl.multiple_of((which_core * Z + which_z) * seg, seg), seg)]

    slot = t // half

    def k_copy(c):
        return remote(
            kvout.at[c], chunk(slot, core, z), k_send.at[c], k_recv.at[slot], tensor=(t % half) * nkv + c
        )

    def kv_here(c):
        return (t % half) * nkv + c == t

    def finish(c):
        @pl.when(z > 0)
        def _():
            r_copy(c, z).wait_recv()
            pown[c, z] = pown[c, z] + right[c, z].astype(F32)

        @pl.when(z < Z - 1)
        def _():
            l_copy(c, z).wait_recv()
            pown[c, z] = pown[c, z] + left[c, z].astype(F32)

        result = pown[c, z].astype(BF16)
        rows = pl.ds(pl.multiple_of((core * Z + z) * seg, seg), seg)

        @pl.when(c >= nkv)
        def _():
            out[c, rows, :] = result
            g_start(c, z)

        @pl.when(c < nkv)
        def _():
            kvout[c] = result

            @pl.when(kv_here(c))
            def _():
                out[slot, rows, :] = result

            @pl.when(jnp.logical_not(kv_here(c)))
            def _():
                k_copy(c).start()

    def g_copy(c, k, there):
        piece = chunk(c, core, k)
        way = 0 if there == 1 else 1
        return remote(
            piece, piece, g_send.at[way, c, k], g_recv.at[c, k], dp=(z + Z + there) % Z * 2 + core
        )

    def f_copy(c, k):
        piece = chunk(c, core, k)
        return remote(piece, piece, f_send.at[c, k], f_recv.at[c, k], dp=partner)

    def g_start(c, k):
        @pl.when((k <= z) & (z < Z - 1))
        def _():
            g_copy(c, k, 1).start()

        @pl.when((k >= z) & (z > 0))
        def _():
            g_copy(c, k, -1).start()

        f_copy(c, k).start()

    def kv_gather(c):
        @pl.when(c < nkv)
        def _():
            source = c * half + t // nkv

            @pl.when(source != t)
            def _():
                pltpu.make_async_copy(kvout.at[0], chunk(c, core, z), k_recv.at[c]).wait()

            g_start(c, z)

    def g_relay(distance):
        def run(c):
            @pl.when(z >= distance)
            def _():
                g_copy(c, z - distance, 1).wait_recv()
                g_start(c, z - distance)

            @pl.when(z + distance < Z)
            def _():
                g_copy(c, z + distance, -1).wait_recv()
                g_start(c, z + distance)

        return run

    stages = [(0, matmuls), (1, pair_sums)]
    lag = 1
    for place in range(1, Z - 1):
        lag += 1
        stages.append((lag, relay(place)))
    lag += 1
    stages.append((lag, finish))
    lag += 1
    stages.append((lag, kv_gather))
    for distance in range(1, Z):
        stages.append((lag + distance - 1, g_relay(distance)))

    def step(i, _):
        for behind, stage in stages:
            @pl.when((i >= behind) & (i < C + behind))
            def _():
                stage(i - behind)

        return 0

    lax.fori_loop(0, C + stages[-1][0], step, 0)

    def drain(c, _):
        p_copy(c).wait_send()
        for k in range(Z):
            f_copy(c, k).wait()

            @pl.when(k > z)
            def _():
                r_copy(c, k).wait_send()

            @pl.when(k < z)
            def _():
                l_copy(c, k).wait_send()

            @pl.when((k <= z) & (z < Z - 1))
            def _():
                g_copy(c, k, 1).wait_send()

            @pl.when((k >= z) & (z > 0))
            def _():
                g_copy(c, k, -1).wait_send()

        return 0

    lax.fori_loop(0, C, drain, 0)
    for c in range(nkv):
        @pl.when(jnp.logical_not(kv_here(c)))
        def _():
            k_copy(c).wait_send()

    for o in range(1, T):
        e_copy(o).wait_send()
        for piece in range(DP):
            x_copy(o, piece).wait_send()
    for o in range(1, DP):
        a_copy(o).wait_send()


def table_by_kernel(embed_table, norm_gain, query_weight, kv_weight):
    T, DP = lax.axis_size("tensor"), lax.axis_size("dp")
    vocab = embed_table.shape[0] * DP
    width = query_weight.shape[1]
    sub = embed_table.shape[0] // T
    nq = query_weight.shape[0] // WIDE
    nkv = kv_weight.shape[0] // WIDE
    C = nq + nkv
    Z = DP // 2
    seg = vocab // DP
    dma = pltpu.SemaphoreType.DMA
    return pl.pallas_call(
        functools.partial(table_kernel, T, DP),
        out_shape=jax.ShapeDtypeStruct((C, vocab, WIDE), BF16),
        in_specs=[pl.BlockSpec(memory_space=pl.ANY)] * 4,
        out_specs=pl.BlockSpec(memory_space=pltpu.VMEM),
        scratch_shapes=[
            pltpu.VMEM(embed_table.shape, BF16),
            pltpu.VMEM((1, norm_gain.shape[0]), F32),
            pltpu.VMEM((T, sub, embed_table.shape[1]), BF16),
            pltpu.VMEM((DP, sub, width), BF16),
            pltpu.VMEM((T, DP, sub, width), BF16),
            pltpu.VMEM((C, WIDE, width), BF16),
            pltpu.VMEM((C, Z * seg, WIDE), F32),
            pltpu.VMEM((C, Z, seg, WIDE), F32),
            pltpu.VMEM((C, Z * seg, WIDE), F32),
            pltpu.VMEM((C, Z, seg, WIDE), BF16),
            pltpu.VMEM((C, Z, seg, WIDE), BF16),
            pltpu.VMEM((C, Z, seg, WIDE), BF16),
            pltpu.VMEM((nkv, seg, WIDE), BF16),
            dma((4,)), dma((T - 1,)), dma((T - 1,)), dma((DP - 1,)), dma((DP - 1,)),
            dma((T - 1, DP)), dma((T - 1, DP)),
            dma((C,)), dma((C,)), dma((C, Z)), dma((C, Z)), dma((C, Z)), dma((C, Z)),
            dma((nkv,)), dma((nkv,)), dma((2, C, Z)), dma((C, Z)), dma((C, Z)), dma((C, Z)),
        ],
        compiler_params=pltpu.CompilerParams(
            collective_id=0, has_side_effects=True, vmem_limit_bytes=56 * 1024 * 1024
        ),
        name="vocab_table",
    )(
        embed_table, norm_gain[None, :], query_weight.reshape(nq, WIDE, width), kv_weight.reshape(nkv, WIDE, width)
    )


def table_by_collectives(embed_table, norm_gain, query_weight, kv_weight, first_kv, kv_count):
    rows = lax.all_gather(embed_table, "tensor", axis=1, tiled=True).astype(F32)
    mean_square = jnp.mean(rows * rows, axis=1, keepdims=True)
    normed_rows = (rows * lax.rsqrt(mean_square + epsilon) * norm_gain[None, :]).astype(BF16)
    normed = lax.all_to_all(normed_rows, "dp", split_axis=1, concat_axis=0, tiled=True)
    kv_grid = lax.all_gather(kv_weight, "tensor", axis=0, tiled=True).reshape(2, KV_HEADS, HD, -1)
    kv_rows = lax.dynamic_slice_in_dim(kv_grid, first_kv, kv_count, 1).reshape(2, kv_count * HD, -1)
    kv_rows = jnp.pad(kv_rows, ((0, 0), (0, -kv_count * HD % WIDE), (0, 0))).reshape(-1, kv_rows.shape[2])
    weights = jnp.concatenate([kv_rows, query_weight], axis=0)
    summed = lax.psum_scatter(contract_last(normed, weights), "dp", scatter_dimension=0, tiled=True)
    table = lax.all_gather(summed.astype(BF16), "dp", axis=0, tiled=True)
    return table.reshape(table.shape[0], -1, WIDE).transpose(1, 0, 2)


def on_device(token_ids, seq_lengths, embed_table, norm_gain, query_weight, kv_weight):
    tok_rows = token_ids.shape[0]
    tensor_count, dp_count = lax.axis_size("tensor"), lax.axis_size("dp")
    heads_here = query_weight.shape[0] // HD
    group_size = HEADS // KV_HEADS
    kv_count = max(1, heads_here // group_size)
    per_dp = embed_table.shape[0]
    vocab = per_dp * dp_count
    sub = per_dp // tensor_count
    if sub % 16 == 0 and kv_count * HD == WIDE and tensor_count == 4 and dp_count % 2 == 0:
        table = table_by_kernel(embed_table, norm_gain, query_weight, kv_weight)
    else:
        sub = 0
        first_kv = lax.axis_index("tensor") * heads_here // group_size
        table = table_by_collectives(embed_table, norm_gain, query_weight, kv_weight, first_kv, kv_count)
    per_group = heads_here // kv_count
    cosine, sine = rope_tables()
    whole = pl.BlockSpec((SEQ, HD), lambda s, j: (0, 0))
    return pl.pallas_call(
        functools.partial(attend_kernel, sub, tensor_count, per_dp, per_group, max(1, kv_count * HD // WIDE)),
        grid=(tok_rows // SEQ, kv_count),
        out_shape=jax.ShapeDtypeStruct((tok_rows, heads_here * HD), BF16),
        in_specs=[
            pl.BlockSpec(memory_space=pltpu.SMEM),
            pl.BlockSpec((1, 1, SEQ), lambda s, j: (s, 0, 0)),
            whole,
            whole,
            pl.BlockSpec(memory_space=pltpu.VMEM),
        ],
        out_specs=pl.BlockSpec((SEQ, per_group * HD), lambda s, j: (s, j)),
        scratch_shapes=[pltpu.VMEM((SEQ, vocab), BF16)],
        name="attend",
    )(seq_lengths, token_ids.reshape(-1, 1, SEQ), cosine, sine, table)


def solution(mesh):
    placed = (P("dp"), P("dp"), P("dp", "tensor"), P(), P("tensor", "dp"), P("tensor", "dp"))
    return jax.shard_map(
        on_device, mesh=mesh, in_specs=placed, out_specs=P("dp", "tensor"), check_vma=False
    )
```

time: 119 us -> 97.4 us (0.82); the launches traced: 119 us -> 95.6 us
  Pallas kernels: 113 us -> 95.6 us
  local copies, waits for them, and re-layouts: 5.96 us -> 0 us
    pallas_call x1, Pallas kernels: 96.3 us -> 82.1 us  [table_by_kernel(): pl.pallas_call(functools.partial(table_kernel, T, DP), out_shape=jax.Shap...]
    unnamed x8 -> x0, local copies, waits for them, and re-layouts: 4.43 us -> none
    pallas_call x1, Pallas kernels: 16.9 us -> 13.5 us  [on_device(): pl.pallas_call(functools.partial(attend_kernel, sub, tensor_count, per_dp...]
    broadcast_in_dim x1 -> x0, local copies, waits for them, and re-layouts: 1.53 us -> none  [on_device(): token_ids[:, None]]
where the time goes in v3:
time: 97.4 us; the launch traced here: 95.6 us
  Pallas kernels  95.6 us (98%)
    pallas_call x1, Pallas kernels, table_by_kernel(): pl.pallas_call(functools.partial(table_kernel, T, DP), out_shape=jax.Shap...  82.1 us
    pallas_call x1, Pallas kernels, on_device(): pl.pallas_call(functools.partial(attend_kernel, sub, tensor_count, per_dp...  13.5 us

profile of v3, /device:TPU:0, one launch (start us, length us, event | category | flops | bytes accessed | tf_op | source)
XLA Modules:
  0.0 95.6 jit_solution(11473479603376613787)
XLA Ops:
  0.0 82.1 %vocab_table.1.table = bf16[10,512,256]{2,1,0:T(8,128)(2,1)} custom-call(bf16[64,2048]{1,0:T(8,128)(2,1)} %emb_in.1, f32[1,8192]{1,0:T(1,128)} %bitcast.6, bf16[8,256,1024]{2,1,0:T(8,128)(2,1)} %bitcast.4, bf16[2,256,1024]{2,1,0:T(8,128)(2,1)} %bitcast.5), custom_call_target="tpu_custom_call" | custom-call | tf_op jit(solution)/shard_map/vocab_table/pallas_call | solution.py:388
  82.1 13.5 %attend.1 = bf16[512,2048]{1,0:T(8,128)(2,1)} custom-call(s32[2]{0:T(128)} %len_ref.1, s32[2,1,256]{2,1,0:T(1,128)} %bitcast.7, f32[256,128]{1,0:T(8,128)} %constant.4.clone.cos_ref, f32[256,128]{1,0:T(8,128)} %constant.5.clone.sin_ref, bf16[10,512,256]{2,1,0:T(8,128)(2,1)} %vocab_table.1.table), custom_call_target="tpu_custom_call" | custom-call | tf_op jit(solution)/shard_map/attend/pallas_call | solution.py:453

commit v4 on v3

--- a/solution.py
+++ b/solution.py
@@ -64,26 +64,32 @@
 
     keys = rotate(jnp.dot(one_hot, table[part, :, lane], preferred_element_type=F32))
     values = jnp.dot(one_hot, table[nkv + part, :, lane], preferred_element_type=F32).astype(BF16)
-    row = lax.broadcasted_iota(jnp.int32, (SEQ, SEQ), 0)
-    column = lax.broadcasted_iota(jnp.int32, (SEQ, SEQ), 1)
-    allowed = (column <= row) & (column < length)
+    parts = []
+    for first, last in ((0, SEQ // 2), (SEQ // 2, SEQ)):
+        row = lax.broadcasted_iota(jnp.int32, (last - first, last), 0) + first
+        column = lax.broadcasted_iota(jnp.int32, (last - first, last), 1)
+        parts.append((first, last, (column <= row) & (column < length)))
     for block in range(heads * HD // WIDE):
-        picked = jnp.dot(one_hot, table[2 * nkv + group * (heads * HD // WIDE) + block], preferred_element_type=F32)
+        picked = jnp.dot(
+            one_hot, table[2 * nkv + group * (heads * HD // WIDE) + block], preferred_element_type=F32
+        )
         for inner in range(WIDE // HD):
             queries = rotate(picked[:, inner * HD : (inner + 1) * HD])
-            scores = contract_last(queries, keys) * (1.0 / math.sqrt(HD))
-            scores = jnp.where(allowed, scores, -1e30)
-            exponent = jnp.exp(scores - jnp.max(scores, axis=1, keepdims=True))
-            total = jnp.sum(exponent, axis=1, keepdims=True)
-            probs = (exponent * (1.0 / total)).astype(BF16)
             start = block * WIDE + inner * HD
-            out_ref[:, start : start + HD] = jnp.dot(
-                probs, values, preferred_element_type=F32
-            ).astype(BF16)
+            for first, last, allowed in parts:
+                scores = contract_last(queries[first:last], keys[:last]) * (1.0 / math.sqrt(HD))
+                scores = jnp.where(allowed, scores, -1e30)
+                exponent = jnp.exp(scores - jnp.max(scores, axis=1, keepdims=True))
+                total = jnp.sum(exponent, axis=1, keepdims=True)
+                probs = (exponent * (1.0 / total)).astype(BF16)
+                out_ref[first:last, start : start + HD] = jnp.dot(
+                    probs, values[:last], preferred_element_type=F32
+                ).astype(BF16)
 
 
 def table_kernel(
-    T, DP, emb_in, gain_in, wq, kvw, out,
+    T, DP, per_dp, emb_in, gain_in, wq, kvw, len_ref, id_ref, cos_ref, sin_ref, att,
+    out, picker, keys, values,
     emb, gain, rows_in, nrm, xt, wbuf, psend, pown, precv, zsend, right, left, kvout,
     w_sem, e_send, e_recv, a_send, a_recv, x_send, x_recv,
     p_send, p_recv, r_send, r_recv, l_send, l_recv, k_send, k_recv, g_send, g_recv, f_send, f_recv,
@@ -114,6 +120,13 @@
     )
     for load in loads:
         load.start()
+    vocab = out.shape[1]
+    seqs = id_ref.shape[0]
+    for q in range(seqs):
+        ids = id_ref[q]
+        ids = ((ids % per_dp) // sub) * (vocab // T) + (ids // per_dp) * sub + ids % sub
+        hits = jnp.where(ids == lax.broadcasted_iota(jnp.int32, (vocab, SEQ), 0), 1.0, 0.0)
+        picker[q] = hits.T.astype(BF16)
 
     barrier = pltpu.get_barrier_semaphore()
     for o in range(1, T):
@@ -327,6 +340,53 @@
     for distance in range(1, Z):
         stages.append((lag + distance - 1, g_relay(distance)))
 
+    def rotate(x):
+        return (x * cos_ref[...] + pltpu.roll(x, HD // 2, 1) * sin_ref[...]).astype(BF16)
+
+    lanes = WIDE // HD
+
+    def attend(c):
+        for k in range(Z):
+            f_copy(c, k).wait_recv()
+
+        @pl.when(c == 0)
+        def _():
+            for q in range(seqs):
+                picked = jnp.dot(picker[q], out[0], preferred_element_type=F32)
+                for g in range(lanes):
+                    keys[g, q] = rotate(picked[:, g * HD : (g + 1) * HD])
+
+        @pl.when(c == 1)
+        def _():
+            for q in range(seqs):
+                picked = jnp.dot(picker[q], out[1], preferred_element_type=F32).astype(BF16)
+                for g in range(lanes):
+                    values[g, q] = picked[:, g * HD : (g + 1) * HD]
+
+        @pl.when(c >= nkv)
+        def _():
+            block = c - nkv
+            group = block // (nq // lanes)
+            for q in range(seqs):
+                picked = jnp.dot(picker[q], out[c], preferred_element_type=F32)
+                for inner in range(lanes):
+                    queries = rotate(picked[:, inner * HD : (inner + 1) * HD])
+                    lane = pl.ds(pl.multiple_of(block * WIDE + inner * HD, HD), HD)
+                    for first, last in ((0, SEQ // 2), (SEQ // 2, SEQ)):
+                        row = lax.broadcasted_iota(jnp.int32, (last - first, last), 0) + first
+                        column = lax.broadcasted_iota(jnp.int32, (last - first, last), 1)
+                        allowed = (column <= row) & (column < len_ref[q])
+                        scores = contract_last(queries[first:last], keys[group, q, :last]) * (1.0 / math.sqrt(HD))
+                        scores = jnp.where(allowed, scores, -1e30)
+                        exponent = jnp.exp(scores - jnp.max(scores, axis=1, keepdims=True))
+                        total = jnp.sum(exponent, axis=1, keepdims=True)
+                        probs = (exponent * (1.0 / total)).astype(BF16)
+                        att[q * SEQ + first : q * SEQ + last, lane] = jnp.dot(
+                            probs, values[group, q, :last], preferred_element_type=F32
+                        ).astype(BF16)
+
+    stages.append((stages[-1][0] + 1, attend))
+
     def step(i, _):
         for behind, stage in stages:
             @pl.when((i >= behind) & (i < C + behind))
@@ -340,7 +400,7 @@
     def drain(c, _):
         p_copy(c).wait_send()
         for k in range(Z):
-            f_copy(c, k).wait()
+            f_copy(c, k).wait_send()
 
             @pl.when(k > z)
             def _():
@@ -374,7 +434,7 @@
         a_copy(o).wait_send()
 
 
-def table_by_kernel(embed_table, norm_gain, query_weight, kv_weight):
+def attend_by_kernel(token_ids, seq_lengths, embed_table, norm_gain, query_weight, kv_weight):
     T, DP = lax.axis_size("tensor"), lax.axis_size("dp")
     vocab = embed_table.shape[0] * DP
     width = query_weight.shape[1]
@@ -384,13 +444,20 @@
     C = nq + nkv
     Z = DP // 2
     seg = vocab // DP
+    seqs = token_ids.shape[0] // SEQ
     dma = pltpu.SemaphoreType.DMA
     return pl.pallas_call(
-        functools.partial(table_kernel, T, DP),
-        out_shape=jax.ShapeDtypeStruct((C, vocab, WIDE), BF16),
-        in_specs=[pl.BlockSpec(memory_space=pl.ANY)] * 4,
+        functools.partial(table_kernel, T, DP, embed_table.shape[0]),
+        out_shape=jax.ShapeDtypeStruct((token_ids.shape[0], nq * WIDE), BF16),
+        in_specs=[pl.BlockSpec(memory_space=pl.ANY)] * 4
+        + [pl.BlockSpec(memory_space=pltpu.SMEM)]
+        + [pl.BlockSpec(memory_space=pltpu.VMEM)] * 3,
         out_specs=pl.BlockSpec(memory_space=pltpu.VMEM),
         scratch_shapes=[
+            pltpu.VMEM((C, vocab, WIDE), BF16),
+            pltpu.VMEM((seqs, SEQ, vocab), BF16),
+            pltpu.VMEM((WIDE // HD, seqs, SEQ, HD), BF16),
+            pltpu.VMEM((WIDE // HD, seqs, SEQ, HD), BF16),
             pltpu.VMEM(embed_table.shape, BF16),
             pltpu.VMEM((1, norm_gain.shape[0]), F32),
             pltpu.VMEM((T, sub, embed_table.shape[1]), BF16),
@@ -412,9 +479,10 @@
         compiler_params=pltpu.CompilerParams(
             collective_id=0, has_side_effects=True, vmem_limit_bytes=56 * 1024 * 1024
         ),
-        name="vocab_table",
+        name="table_attend",
     )(
-        embed_table, norm_gain[None, :], query_weight.reshape(nq, WIDE, width), kv_weight.reshape(nkv, WIDE, width)
+        embed_table, norm_gain[None, :], query_weight.reshape(nq, WIDE, width), kv_weight.reshape(nkv, WIDE, width),
+        seq_lengths, token_ids.reshape(-1, 1, SEQ), *rope_tables()
     )
 
 
@@ -442,11 +510,10 @@
     vocab = per_dp * dp_count
     sub = per_dp // tensor_count
     if sub % 16 == 0 and kv_count * HD == WIDE and tensor_count == 4 and dp_count % 2 == 0:
-        table = table_by_kernel(embed_table, norm_gain, query_weight, kv_weight)
-    else:
-        sub = 0
-        first_kv = lax.axis_index("tensor") * heads_here // group_size
-        table = table_by_collectives(embed_table, norm_gain, query_weight, kv_weight, first_kv, kv_count)
+        return attend_by_kernel(token_ids, seq_lengths, embed_table, norm_gain, query_weight, kv_weight)
+    sub = 0
+    first_kv = lax.axis_index("tensor") * heads_here // group_size
+    table = table_by_collectives(embed_table, norm_gain, query_weight, kv_weight, first_kv, kv_count)
     per_group = heads_here // kv_count
     cosine, sine = rope_tables()
     whole = pl.BlockSpec((SEQ, HD), lambda s, j: (0, 0))

time: 97.4 us -> 96.8 us (level)
  Pallas kernels: 95.6 us -> 92.1 us
  local copies, waits for them, and re-layouts: 0 us -> 3.16 us
    pallas_call x2 -> x1, Pallas kernels: 95.6 us -> 92.1 us  [attend_by_kernel(): pl.pallas_call(functools.partial(table_kernel, T, DP, embed_table.shape[0...]
    unnamed x0 -> x1, local copies, waits for them, and re-layouts: none -> 3.16 us
where the time goes in v4:
time: 96.8 us; the launch traced here: 95.3 us
  Pallas kernels  92.1 us (95%)
  local copies, waits for them, and re-layouts  3.16 us (3%)
    pallas_call x1, Pallas kernels, attend_by_kernel(): pl.pallas_call(functools.partial(table_kernel, T, DP, embed_table.shape[0...  92.1 us
    unnamed x1, local copies, waits for them, and re-layouts  3.16 us

profile of v4, /device:TPU:0, one launch (start us, length us, event | category | flops | bytes accessed | tf_op | source)
XLA Modules:
  0.0 95.3 jit_solution(7241366029161650222)
XLA Ops:
  0.0 92.1 %table_attend.1 = bf16[512,2048]{1,0:T(8,128)(2,1)} custom-call(bf16[64,2048]{1,0:T(8,128)(2,1)} %emb_in.1, f32[1,8192]{1,0:T(1,128)} %bitcast.6, bf16[8,256,1024]{2,1,0:T(8,128)(2,1)} %bitcast.4, bf16[2,256,1024]{2,1,0:T(8,128)(2,1)} %bitcast.5, s32[2]{0:T(128)} %len_ref.1, s32[2,1,256]{2,1,0:T(1,128)} %bitcast.7, f32[256,128]{1,0:T(8,128)} %constant.4.clone.cos_ref, ...), custom_call_target="tpu_custom_call" | custom-call | tf_op jit(solution)/shard_map/table_attend/pallas_call | solution.py:449
  92.1 3.2 %copy.10 = bf16[512,2048]{1,0:T(8,128)(2,1)} copy(bf16[512,2048]{1,0:T(8,128)(2,1)} %table_attend.1) | data formatting | bytes 4194304
